TPU v7x, 128 devices: a whole 4x4x4 slice. The times are simulated.
128 devices in a mesh: row: 16 (over y_lo, z, core), col: 8 (over y_hi, x).
Axes of the slice: x: 4, y: 4 (y_hi: 2, y_lo: 2; y = y_hi * 2 + y_lo), z: 4, core: 2. Of those that a mesh axis runs over, the one named last changes fastest.
Arguments:
- policy_rows: bfloat16 [4096, 131072], P(('row', 'col')), may hold values from 0 to 1, as said below
- action_rows: bfloat16 [4096, 16, 8, 1024], P('row', None, 'col'), may hold values from 0 to 1, as said below
- prev_values: float32 [32, 131072], P(None, ('row', 'col')), may hold values from -2000 to 2000
- action_costs: float32 [32, 8, 4096], P(None, None, ('row', 'col')), may hold values from 0 to 2
- policy: int32 [4096], P(('row', 'col')), may hold values from 0 to 7
- target_costs: float32 [32, 4096], P(None, ('row', 'col')), may hold values from 0 to 2
- anchor: int32 [1], replicated, may hold values from 0 to 4095
Outputs:
- relative: float32 [32, 4096], P(None, ('row', 'col'))
- q_values: float32 [32, 4096], P(None, ('row', 'col'))
Inputs may be any that keep to these rules, and one draw needn't show every extreme that they name: `policy_rows`: entries are nonnegative transition probabilities, each row sums to about one. `action_rows`: entries are nonnegative transition probabilities, each row sums to about one.
All inputs are finite; a program needn't handle non-finite values.
Results may differ from a plain program's by a relative error of at most 0.0024.
Values may be sent and summed in bfloat16 or wider, within the bound.
A program may use at most 128 MiB of HBM per device.

v0:
```python
import jax
import jax.numpy as jnp
from jax import lax
from jax.sharding import PartitionSpec as P


def local(policy_rows, action_rows, prev_values, action_costs, policy, target_costs, anchor):
    scenarios = prev_values.shape[0]
    shard_len = prev_values.shape[1]
    pi_count = policy_rows.shape[0]
    row_count = lax.axis_size("row")
    col_count = lax.axis_size("col")
    col_index = lax.axis_index("col")
    linear = lax.axis_index("row") * col_count + col_index
    r_total = pi_count * row_count * col_count
    prev_bf16 = prev_values.astype(jnp.bfloat16)
    one_hot = (
        policy[None, :] == jnp.arange(action_costs.shape[1], dtype=jnp.int32)[:, None]
    ).astype(jnp.float32)
    policy_cost = jnp.sum(action_costs * one_hot[None, :, :], axis=1)
    swept_sum = lax.dot_general(
        lax.all_gather(prev_bf16, ("row", "col"), axis=1, tiled=True),
        policy_rows,
        (((1,), (1,)), ((), ())),
        preferred_element_type=jnp.float32,
    )
    fresh_vals = policy_cost + swept_sum
    fresh_all = lax.all_gather(fresh_vals, ("row", "col"), axis=1, tiled=True)
    row_pos = linear * pi_count + jnp.arange(pi_count, dtype=jnp.int32)
    picked = jnp.sum(jnp.where(row_pos[None, :] == anchor[0], fresh_vals, 0.0), axis=1)
    gain_value = lax.psum(picked, ("row", "col"))
    relative = fresh_vals - gain_value[:, None]
    relative_all = (fresh_all - gain_value[:, None]).astype(jnp.bfloat16)
    fresh_wide = jnp.concatenate(
        [relative_all, jnp.zeros((scenarios, shard_len), jnp.bfloat16)], axis=1
    )
    start = linear * shard_len
    global_pos = start + jnp.arange(shard_len, dtype=jnp.int32)
    replaced = lax.dynamic_slice_in_dim(fresh_wide, jnp.minimum(start, r_total), shard_len, 1)
    own_block = jnp.where(global_pos[None, :] < r_total, replaced, prev_bf16)
    column = lax.all_gather(own_block, "row", axis=1, tiled=True)
    act_tile = action_rows.reshape(action_rows.shape[0], row_count * shard_len)
    partial_value = lax.dot_general(
        column, act_tile, (((1,), (1,)), ((), ())), preferred_element_type=jnp.float32
    )
    summed_q = lax.psum_scatter(partial_value, "col", scatter_dimension=1, tiled=True)
    q_values = target_costs + summed_q - gain_value[:, None]
    return (relative, q_values)


def solution(mesh):
    in_specs = (
        P(("row", "col"), None),
        P("row", None, "col", None),
        P(None, ("row", "col")),
        P(None, None, ("row", "col")),
        P(("row", "col")),
        P(None, ("row", "col")),
        P(),
    )
    out_specs = (P(None, ("row", "col")), P(None, ("row", "col")))
    return jax.shard_map(local, mesh=mesh, in_specs=in_specs, out_specs=out_specs, check_vma=False)
```

profile of v0, /device:TPU:24, one launch (start us, length us, event | category | flops | bytes accessed | tf_op | source)
XLA Modules:
  0.0 882.2 jit_solution(14728359260927913879)
XLA Ops:
  7.2 0.0 all-gather.3.cloned.1.call-start
  7.2 1.7 copy.14
  9.0 0.0 all-gather.3.cloned.1.call-update
  9.0 0.0 all-gather.5.cloned.1.call-start
  9.7 0.7 fusion.1
  10.4 0.9 multiply_reduce_fusion
  11.3 0.1 copy.15
  11.4 0.0 copy-start
  11.4 342.8 %all-gather.3.cloned.1.call-done = bf16[32,131072]{0,1:T(8,128)(2,1)} async-done(((bf16[32,1024]{0,1:T(8,128)(2,1)}), bf16[32,131072]{0,1:T(8,128)(2,1)}) %all-gather.3.cloned.1.call-update) | async-done | bytes 8388624 | tf_op jit(solution)/shard_map/all_gather | solution.py:22
  354.2 15.7 %select_reduce_fusion = (f32[32]{0:T(128)S(1)}, f32[32,32]{0,1:T(8,128)S(1)}) fusion(pred[32]{0:T(512)(128)(4,1)S(1)} %add_compare_fusion.1, f32[32,32]{0,1:T(8,128)S(1)} %copy.15, bf16[32,131072]{1,0:T(8,128)(2,1)} %param.7, bf16[32,131072]{0,1:T(8,128)(2,1)} %all-gather.3.cloned.1.call-done), kind=kOutput, calls=%fused_computation.6 | convolution fusion | flops 268438496 | bytes 16785568 | tf_op jit(solution)/shard_map/dot_general | solution.py:21
  369.9 293.4 %all_gather.10 = f32[32,4096]{0,1:T(8,128)S(1)} all-gather(f32[32,32]{0,1:T(8,128)S(1)} %get-tuple-element.9), channel_id=1, replica_groups=mesh['row'=16,'col'=8] {'row','col'}, dimensions={1}, use_global_device_ids=true | all-gather | bytes 528384 | tf_op jit(solution)/shard_map/all_gather | solution.py:28
  663.3 95.0 %psum.7 = f32[32]{0:T(128)S(1)} all-reduce(f32[32]{0:T(128)S(1)} %get-tuple-element.8), channel_id=1, replica_groups=mesh['row'=16,'col'=8] {'row','col'}, use_global_device_ids=true, to_apply=%region_2.3 | all-reduce | flops 32 | bytes 256 | tf_op jit(solution)/shard_map/psum | solution.py:31
  758.3 0.1 subtract_convert_fusion
  758.4 0.0 copy-done
  758.4 1.2 fusion
  759.6 0.0 all-gather.5.cloned.1.call-update
  759.6 0.2 reduce-scatter.2.cloned.1.call-start
  759.9 15.6 %copy.21 = bf16[32,8,16,1024]{3,1,2,0:T(8,128)(2,1)} copy(bf16[32,8,16,1024]{3,2,1,0:T(8,128)(2,1)} %bitcast.11) | data formatting | bytes 16777216
  775.5 20.2 %all-gather.5.cloned.1.call-done = bf16[32,16384]{0,1:T(8,128)(2,1)} async-done(((bf16[32,1024]{0,1:T(8,128)(2,1)}), bf16[32,16384]{0,1:T(8,128)(2,1)}) %all-gather.5.cloned.1.call-update) | async-done | bytes 1048592 | tf_op jit(solution)/shard_map/all_gather | solution.py:41
  795.7 0.0 copy-start.1
  795.7 7.6 fusion.2
  803.3 0.0 reduce-scatter.2.cloned.1.call-update
  803.3 0.0 copy-done.1
  803.3 0.1 copy.17
  803.4 70.2 %reduce-scatter.2.cloned.1.call-done = f32[32,32]{0,1:T(8,128)} async-done(((f32[32,256]{0,1:T(8,128)}), f32[32,32]{0,1:T(8,128)}) %reduce-scatter.2.cloned.1.call-update) | async-done | bytes 4112 | tf_op jit(solution)/shard_map/reduce_scatter | solution.py:46
  873.6 0.7 add_subtract_fusion
  874.3 0.7 copy.18
  875.0 0.7 copy.19
  (2 shorter events, 0.0 us)
Async XLA Ops:
  7.2 347.0 %all-gather.3.cloned.1.call-start = ((), (), s32[]{:S(2)}) async-start(), calls=%async_computation.1 | async-start | bytes 33816576 | tf_op jit(solution)/shard_map/all_gather | solution.py:22
  9.0 786.7 %all-gather.5.cloned.1.call-start = ((), (), s32[]{:S(2)}) async-start(), calls=%async_computation.2 | async-start | bytes 4456448 | tf_op jit(solution)/shard_map/all_gather | solution.py:41
  11.4 747.0 %copy-start = (bf16[32,1024]{0,1:T(8,128)(2,1)S(1)}, bf16[32,1024]{0,1:T(8,128)(2,1)}, u32[]{:S(2)}) copy-start(bf16[32,1024]{0,1:T(8,128)(2,1)} %copy.14) | copy-start | bytes 196612
  759.6 114.0 %reduce-scatter.2.cloned.1.call-start = ((), (), s32[]{:S(2)}) async-start(), calls=%async_computation.3 | async-start | bytes 147456 | tf_op jit(solution)/shard_map/reduce_scatter | solution.py:46
  795.7 7.6 copy-start.1
Sparse Core Ops, SparseCore 0:
  9.7 344.4 all-gather.2
  759.8 35.9 all-gather.4
  803.4 70.1 reduce-scatter.1
where the time goes:
time: 884 us; the launch traced here: 882 us
  waiting for transfers between devices  433 us (49%)
  blocking collectives  388 us (44%)
  matrix products  23.3 us (3%)
  local copies, waits for them, and re-layouts  18.9 us (2%)
  between operations  14.4 us (2%)
    all_gather x1, waiting for transfers between devices, local(): lax.all_gather(prev_bf16, ('row', 'col'), axis=1, tiled=True)  343 us
    all_gather x1, blocking collectives, local(): fresh_all = lax.all_gather(fresh_vals, ('row', 'col'), axis=1, tiled=True)  293 us
    psum x1, blocking collectives, local(): gain_value = lax.psum(picked, ('row', 'col'))  95 us
    reduce_scatter x1, waiting for transfers between devices, local(): lax.psum_scatter(partial_value, 'col', scatter_dimension=1, tiled=True)  70.2 us
    all_gather x1, waiting for transfers between devices, local(): column = lax.all_gather(own_block, 'row', axis=1, tiled=True)  20.2 us
    unnamed x9, local copies, waits for them, and re-layouts  18.8 us
  transfers between devices with their start and end apart: 3, of which 3 were waited for; matrix products, arithmetic and copies ran while one was open for 2% of the time, Pallas kernels for 0%

commit v1 on v0

v1 whole, which is shorter than its diff:
```python
import functools

import jax
import jax.numpy as jnp
from jax import lax
from jax.experimental import pallas as pl
from jax.experimental.pallas import tpu as pltpu
from jax.sharding import PartitionSpec as P

MESH = pl.DeviceIdType.MESH
F32, BF16 = jnp.float32, jnp.bfloat16
STEPS = ((1, 0, 0), (3, 0, 0), (0, 1, 0), (0, 3, 0), (0, 0, 1), (0, 0, 3))
PLAN = (
    (0, 448, 512, 576, 640, 320),
    (384, 64, 128, 192, 256, 704),
    (),
    (),
    (385, 452, 131, 195, 641, 708),
    (1, 67, 129, 579, 268, 323),
    (388, 65, 513, 588, 652, 720),
    (3, 76, 176, 204, 688, 752),
    (4, 112, 514, 578, 657, 327),
    (13, 496, 519, 194, 692, 756),
    (397, 461, 532, 624, 273, 724),
    (404, 497, 564, 241, 308, 380),
    (15, 462, 134, 224, 288, 328),
    (6, 503, 179, 221, 660, 759),
    (399, 508, 180, 637, 664, 352),
    (8, 78, 160, 255, 305, 340),
    (402, 510, 567, 590, 309, 764),
    (25, 502, 551, 253, 281, 727),
    (22, 505, 161, 227, 665, 735),
    (403, 126, 151, 210, 289, 356),
    (5, 123, 164, 254, 676, 763),
    (395, 511, 169, 589, 689, 733),
    (413, 89, 550, 208, 297, 745),
)
LATENCY = 4


def plan_of():
    ready = {(half, 0): 0 for half in range(2)}
    sends = []
    for step, row in enumerate(PLAN):
        line = []
        for entry in row:
            half, rest = divmod(entry, 384)
            way, code = divmod(rest, 64)
            place = (code // 16, code // 4 % 4, code % 4)
            to = tuple((a + b) % 4 for a, b in zip(place, STEPS[way]))
            target = to[0] * 16 + to[1] * 4 + to[2]
            line.append((half, way, code, target))
            ready[half, target] = step + LATENCY
        sends.append(line)
    done = {code: max(ready[0, code], ready[1, code]) for code in range(64)}
    order = sorted(range(64), key=lambda code: (done[code], code))
    slot = {code: n for n, code in enumerate(order)}
    first = max(done[order[4 * g + 3]] - g for g in range(16))
    last = first + 15
    waits = [[] for _ in range(last + 1)]
    for (half, code), when in ready.items():
        if code:
            turn = first + slot[code] // 4
            assert turn >= when, (turn, when)
            uses = [s for s, line in enumerate(sends) for h, _, c, _ in line if (h, c) == (half, code)]
            waits[min(uses + [turn])].append((when, half, slot[code]))
    steps = []
    for step in range(last + 1):
        line = sends[step] if step < len(sends) else []
        steps.append(
            (
                [(h, n) for _, h, n in sorted(waits[step])],
                [(h, way, slot[c], slot[t]) for h, way, c, t in line],
            )
        )
    return order, slot, steps, first


ORDER, SLOT, STEP_PLAN, FIRST = plan_of()


def tile4(x):
    x = x + pltpu.roll(x, 64, 1)
    return x + pltpu.roll(x, 32, 1)


def pack(x, group):
    out = x[0:8]
    for g in range(1, 4):
        out = jnp.where(group[0:8] == g, x[8 * g : 8 * g + 8], out)
    return out


def kernel(
    policy_rows, action_rows, prev, costs, policy, anchor, rel_out, q_out,
    prev_buf, cost_buf, policy_buf, blocks, own_rows, actions, column, first_tile, acc, rest, half_out, half_in,
    packed, gathered, combined, message, arrived,
    in_sem, cost_sem, rows_sem, other_sem, act_sem, recv_sem, col_sem, half_sem, fresh_sem, q_sem, self_sem, send_sem, psend_sem, csend_sem, hsend_sem, fsend_sem, qsend_sem,
):
    row, col = lax.axis_index("row"), lax.axis_index("col")
    core = row % 2
    z = row // 2 % 4
    y_lo = row // 8
    y_hi, x = col // 4, col % 4
    y = y_hi * 2 + y_lo

    def device(x, y, z, core):
        return ((y % 2 * 4 + z) * 2 + core, y // 2 * 4 + x)

    ways = [device((x + a) % 4, (y + b) % 4, (z + c) % 4, core) for a, b, c in STEPS]
    twin = (row + 1 - 2 * core, col)

    load_prev = pltpu.make_async_copy(prev, prev_buf, in_sem.at[0])
    load_prev.start()
    load_costs = pltpu.make_async_copy(costs, cost_buf, cost_sem.at[0])
    load_policy = pltpu.make_async_copy(policy, policy_buf, cost_sem.at[1])
    load_costs.start()
    load_policy.start()

    barrier = pltpu.get_barrier_semaphore()
    for other in ways + [twin]:
        pl.semaphore_signal(barrier, inc=1, device_id=other, device_id_type=MESH)

    def block_of(code, core):
        there = device((x - code // 16) % 4, (y - code // 4 % 4) % 4, (z - code % 4) % 4, core)
        return pl.multiple_of((there[0] * 8 + there[1]) * 1024, 1024)

    def load_rows(n):
        pltpu.make_async_copy(
            policy_rows.at[:, pl.ds(block_of(ORDER[n], core), 1024)], own_rows.at[n, pl.ds(0, 32)], rows_sem.at[n // 4]
        ).start()

    def send_rows(n):
        pltpu.make_async_remote_copy(
            policy_rows.at[:, pl.ds(block_of(ORDER[n], 1 - core), 1024)], own_rows.at[n, pl.ds(32, 32)],
            psend_sem.at[0], other_sem.at[n // 4], device_id=twin, device_id_type=MESH,
        ).start()

    load_prev.wait()
    blocks[0] = prev_buf[...].astype(BF16)
    pl.semaphore_wait(barrier, 7)

    def send_block(half, way, source, target):
        pltpu.make_async_remote_copy(
            blocks.at[source, pl.ds(16 * half, 16)], blocks.at[target, pl.ds(16 * half, 16)],
            send_sem.at[0], recv_sem.at[half * 64 + target], device_id=ways[way], device_id_type=MESH,
        ).start()

    def wait_block(half, n):
        there = blocks.at[n, pl.ds(16 * half, 16)]
        pltpu.make_async_copy(there, there, recv_sem.at[half * 64 + n]).wait()

    def act_copy(n):
        return pltpu.make_async_copy(
            action_rows.at[pl.ds(n * 32, 32)], actions.at[pl.ds(n * 32, 32)], act_sem.at[n]
        )

    acc[...] = jnp.zeros_like(acc)
    lanes = lax.broadcasted_iota(jnp.int32, (64, 128), 1)
    group = lanes // 32

    def column_copies(n):
        y_other, z_other = n // 4, n % 4
        code = (y_lo - y_other + 4) % 4 * 4 + (z - z_other + 4) % 4
        return code, (y_other * 4 + z_other) * 2 + core

    def slot_of(code):
        out = 0
        for c in (0, 1, 2, 3, 4, 5, 6, 7, 12, 13, 14, 15):
            out = out + jnp.where(code == c, SLOT[c], 0)
        return out

    column_step = 1 + max(
        s for s, (waits, _) in enumerate(STEP_PLAN) for _, n in waits if ORDER[n] // 16 == 0 and ORDER[n] // 4 % 4 != 2
    )

    def forward_column():
        for n in range(8):
            code, place = column_copies(n)
            n_slot = slot_of(code)
            pltpu.make_async_remote_copy(
                blocks.at[n_slot], column.at[place], csend_sem.at[0], col_sem.at[1], device_id=twin, device_id_type=MESH
            ).start()
            pltpu.make_async_copy(blocks.at[n_slot], column.at[place], col_sem.at[0]).start()

    def wait_column():
        eight = column.at[pl.ds(0, 8)]
        pltpu.make_async_copy(eight, eight, col_sem.at[0]).wait()
        pltpu.make_async_copy(eight, eight, col_sem.at[1]).wait()

    def policy_group(g):
        mine = own_rows.at[pl.ds(4 * g, 4), pl.ds(0, 32)]
        pltpu.make_async_copy(mine, mine, rows_sem.at[g]).wait()
        twins = own_rows.at[pl.ds(4 * g, 4), pl.ds(32, 32)]
        pltpu.make_async_copy(twins, twins, other_sem.at[g]).wait()
        left = own_rows[pl.ds(4 * g, 4)].reshape(256, 1024)
        right = blocks[pl.ds(4 * g, 4)].reshape(128, 1024)
        acc[...] += lax.dot_general(left, right, (((1,), (1,)), ((), ())), preferred_element_type=F32)

    has_fresh = col < 4

    def action_chunk(n):
        @pl.when(n % 2 == 0)
        def _():
            act_copy(n // 2).wait()

        chunk = actions[pl.ds(16 * n, 16)].reshape(256, 1024)
        values = column[...].reshape(512, 1024)
        out = lax.dot_general(chunk, values, (((1,), (1,)), ((), ())), preferred_element_type=F32)
        out = out.reshape(16, 16, 512)
        here = lax.broadcasted_iota(jnp.int32, (16, 512), 0)
        there = lax.broadcasted_iota(jnp.int32, (16, 512), 1) // 32
        keep = (here == there) & ((there > 0) | jnp.logical_not(has_fresh))
        out = jnp.sum(jnp.where(keep[None], out, 0.0), axis=1)
        out = out[:, 0:128] + out[:, 128:256] + (out[:, 256:384] + out[:, 384:512])
        rest[pl.ds(16 * n, 16)] = tile4(out)

        @pl.when(has_fresh)
        def _():
            pick = (
                lax.broadcasted_iota(jnp.int32, (16, 256), 1) == 16 * lax.broadcasted_iota(jnp.int32, (16, 256), 0)
            ).astype(BF16)
            first_tile[pl.ds(16 * n, 16)] = jnp.dot(pick, chunk, preferred_element_type=F32).astype(BF16)

    last = len(STEP_PLAN) - 1
    chunk_first = max(column_step + 1, 0)
    n_steps = max(last + 1, chunk_first + 16)

    @pl.loop(0, n_steps)
    def _(t):
        for s, (waits, sends) in enumerate(STEP_PLAN):

            @pl.when(t == s)
            def _(s=s, waits=waits, sends=sends):
                for half, n in waits:
                    wait_block(half, n)
                for send in sends:
                    send_block(*send)
                if s == 0:
                    for n in range(64):
                        load_rows(n)
                        send_rows(n)
                    for n in range(8):
                        act_copy(n).start()
                if s == column_step:
                    forward_column()

        @pl.when(t == column_step + 1)
        def _():
            wait_column()

        @pl.when((t >= FIRST) & (t < FIRST + 16))
        def _():
            policy_group(t - FIRST)

        @pl.when((t >= chunk_first) & (t < chunk_first + 16))
        def _():
            action_chunk(t - chunk_first)

    load_costs.wait()
    load_policy.wait()
    chosen = policy_buf[...][:, None, :] == lax.broadcasted_iota(jnp.int32, (1, 8, 32), 1)
    cost = jnp.sum(jnp.where(chosen, cost_buf[...], 0.0), axis=1)
    cost = jnp.concatenate([cost] * 4, axis=0).T

    total = jnp.zeros((64, 128), F32)
    for b in range(4):
        total = total + jnp.where(group == b, acc[64 * b : 64 * b + 64, :], 0.0)
    total = tile4(total)
    half_out[...] = pack(total[32:64], group)
    mine = pack(total[0:32] + cost, group)
    swap = pltpu.make_async_remote_copy(
        half_out, half_in, hsend_sem.at[0], half_sem.at[0], device_id=twin, device_id_type=MESH
    )
    swap.start()
    swap.wait_recv()
    packed[...] = mine + half_in[...]

    place = row % 4 * 8 + col
    target_col = row // 4
    for r in range(16):
        local = (row == r) & (col == target_col)

        @pl.when(local)
        def _():
            pltpu.make_async_copy(packed, gathered.at[place], fresh_sem.at[0]).start()

        @pl.when(jnp.logical_not(local))
        def _(r=r):
            pltpu.make_async_remote_copy(
                packed, gathered.at[place], fsend_sem.at[0], fresh_sem.at[0],
                device_id=(r, target_col), device_id_type=MESH,
            ).start()

    small = group[0:8]

    @pl.when(has_fresh)
    def _():
        pltpu.make_async_copy(gathered, gathered, fresh_sem.at[0]).wait()
        for n in range(32):
            line = gathered[n]
            for g in range(4):
                full = tile4(jnp.where(small == g, line, 0.0))
                high = full.astype(BF16).astype(F32)
                mid = (full - high).astype(BF16).astype(F32)
                low = full - high - mid
                parts = jnp.where(small == 0, high, jnp.where(small == 1, mid, jnp.where(small == 2, low, 1.0)))
                combined[32 * n + 8 * g : 32 * n + 8 * g + 8] = parts.astype(BF16)
        late = jnp.dot(first_tile[...], combined[...], preferred_element_type=F32)
        wide = lax.broadcasted_iota(jnp.int32, (256, 128), 1) // 32
        values = rest[...] + tile4(jnp.where(wide < 3, late, 0.0))
        weights = tile4(jnp.where(wide == 3, late, 0.0))
        state = (
            col * 1024 + lax.broadcasted_iota(jnp.int32, (32, 8, 128), 0) * 32
            + lax.broadcasted_iota(jnp.int32, (32, 8, 128), 2) // 32 * 8
            + lax.broadcasted_iota(jnp.int32, (32, 8, 128), 1)
        )
        gain = jnp.sum(jnp.where(state == anchor[0], gathered[...], 0.0), axis=0)
        gain = tile4(jnp.broadcast_to(jnp.sum(gain, axis=0, keepdims=True), (8, 128)))
        for c in range(8):
            message[c, 0:8] = pack(values[32 * c : 32 * c + 32], small)
            message[c, 8:16] = pack(weights[32 * c : 32 * c + 32], small)
            message[c, 16:24] = gain

    @pl.when(jnp.logical_not(has_fresh))
    def _():
        for c in range(8):
            message[c, 0:8] = pack(rest[32 * c : 32 * c + 32], small)
            message[c, 8:24] = jnp.zeros((16, 128), F32)

    for c in range(8):
        local = col == c

        @pl.when(local)
        def _(c=c):
            pltpu.make_async_copy(message.at[c], arrived.at[col], q_sem.at[0]).start()

        @pl.when(jnp.logical_not(local))
        def _(c=c):
            pltpu.make_async_remote_copy(
                message.at[c], arrived.at[col], qsend_sem.at[0], q_sem.at[0], device_id=(row, c), device_id_type=MESH
            ).start()
    pltpu.make_async_copy(arrived, arrived, q_sem.at[0]).wait()
    total = arrived[0]
    for c in range(1, 8):
        total = total + arrived[c]
    gain = total[16:24]
    rel_out[...] = packed[...] - gain
    q_out[...] = total[0:8] - gain * total[8:16] - gain

    sent = blocks.at[pl.ds(0, 63)]
    pltpu.make_async_copy(sent, sent, send_sem.at[0]).wait()
    given = own_rows.at[:, pl.ds(32, 32)]
    pltpu.make_async_copy(given, given, psend_sem.at[0]).wait()
    eight = column.at[pl.ds(0, 8)]
    pltpu.make_async_copy(eight, eight, csend_sem.at[0]).wait()
    swap.wait_send()

    @pl.when(col == target_col)
    def _():
        part = gathered.at[pl.ds(0, 15)]
        pltpu.make_async_copy(part, part, fsend_sem.at[0]).wait()

    @pl.when(col != target_col)
    def _():
        part = gathered.at[pl.ds(0, 16)]
        pltpu.make_async_copy(part, part, fsend_sem.at[0]).wait()

    part = arrived.at[pl.ds(0, 7)]
    pltpu.make_async_copy(part, part, qsend_sem.at[0]).wait()


def local(policy_rows, action_rows, prev_values, action_costs, policy, target_costs, anchor):
    any_spec = pl.BlockSpec(memory_space=pl.ANY)
    dma = pltpu.SemaphoreType.DMA
    relative, values = pl.pallas_call(
        kernel,
        out_shape=[jax.ShapeDtypeStruct((8, 128), F32)] * 2,
        in_specs=[any_spec] * 5 + [pl.BlockSpec(memory_space=pltpu.SMEM)],
        out_specs=[pl.BlockSpec(memory_space=pltpu.VMEM)] * 2,
        scratch_shapes=[
            pltpu.VMEM((32, 1024), F32),
            pltpu.VMEM((32, 8, 32), F32),
            pltpu.VMEM((1, 32), jnp.int32),
            pltpu.VMEM((64, 32, 1024), BF16),
            pltpu.VMEM((64, 64, 1024), BF16),
            pltpu.VMEM((256, 16, 1024), BF16),
            pltpu.VMEM((16, 32, 1024), BF16),
            pltpu.VMEM((256, 1024), BF16),
            pltpu.VMEM((256, 128), F32),
            pltpu.VMEM((256, 128), F32),
            pltpu.VMEM((8, 128), F32),
            pltpu.VMEM((8, 128), F32),
            pltpu.VMEM((8, 128), F32),
            pltpu.VMEM((32, 8, 128), F32),
            pltpu.VMEM((1024, 128), BF16),
            pltpu.VMEM((8, 24, 128), F32),
            pltpu.VMEM((8, 24, 128), F32),
            dma((1,)), dma((2,)), dma((16,)), dma((16,)), dma((8,)), dma((128,)), dma((2,)), dma((1,)), dma((1,)),
            dma((1,)), dma((1,)), dma((1,)), dma((1,)), dma((1,)), dma((1,)), dma((1,)), dma((1,)),
        ],
        compiler_params=pltpu.CompilerParams(
            collective_id=0, has_side_effects=True, vmem_limit_bytes=60 * 1024 * 1024
        ),
    )(
        policy_rows,
        action_rows.reshape(action_rows.shape[0], 16, 1024),
        prev_values,
        action_costs,
        policy.reshape(1, 32),
        anchor,
    )

    def spread(x):
        return x.reshape(8, 4, 32).transpose(2, 1, 0).reshape(32, 32)

    return spread(relative), spread(values) + target_costs


def solution(mesh):
    in_specs = (
        P(("row", "col"), None),
        P("row", None, "col", None),
        P(None, ("row", "col")),
        P(None, None, ("row", "col")),
        P(("row", "col")),
        P(None, ("row", "col")),
        P(),
    )
    out_specs = (P(None, ("row", "col")), P(None, ("row", "col")))
    return jax.shard_map(local, mesh=mesh, in_specs=in_specs, out_specs=out_specs, check_vma=False)
```

time: 884 us -> 74.1 us (0.08)
  waiting for transfers between devices: 433 us -> 0 us
  blocking collectives: 388 us -> 0 us
  Pallas kernels: 0 us -> 69.6 us
  matrix products: 23.3 us -> 0 us
  local copies, waits for them, and re-layouts: 18.9 us -> 2.96 us
  between operations: 14.4 us -> 1.3 us
    all_gather x2 -> x0, waiting for transfers between devices: 363 us -> none  [the longest x1 343 us: local(): lax.all_gather(prev_bf16, ('row', 'col'), axis=1, tiled=True)]
    all_gather x1 -> x0, blocking collectives: 293 us -> none  [local(): fresh_all = lax.all_gather(fresh_vals, ('row', 'col'), axis=1, tiled=True)]
    psum x1 -> x0, blocking collectives: 95 us -> none  [local(): gain_value = lax.psum(picked, ('row', 'col'))]
    reduce_scatter x1 -> x0, waiting for transfers between devices: 70.2 us -> none  [local(): lax.psum_scatter(partial_value, 'col', scatter_dimension=1, tiled=True)]
    pallas_call x0 -> x1, Pallas kernels: none -> 69.6 us  [local(): pl.pallas_call(kernel, out_shape=[jax.ShapeDtypeStruct((8, 128), F32)] *...]
    dot_general x2 -> x0, matrix products: 23.3 us -> none  [the longest x1 15.7 us: local(): lax.dot_general(lax.all_gather(prev_bf16, ('row', 'col'), axis=1, tiled=T...]
    unnamed x9 -> x5, local copies, waits for them, and re-layouts: 18.8 us -> 1.45 us
  transfers between devices with their start and end apart: 3 -> 0, of which waited for: 3 -> 0; matrix products, arithmetic and copies ran while one was open for 2% -> 0% of each run, Pallas kernels for 0% -> 0%
where the time goes in v1:
time: 74.1 us; the launch traced here: 73.9 us
  Pallas kernels  69.6 us (94%)
  local copies, waits for them, and re-layouts  2.96 us (4%)
  between operations  1.3 us (2%)
    pallas_call x1, Pallas kernels, local(): pl.pallas_call(kernel, out_shape=[jax.ShapeDtypeStruct((8, 128), F32)] *...  69.6 us
    reshape x3, local copies, waits for them, and re-layouts, spread(): return x.reshape(8, 4, 32).transpose(2, 1, 0).reshape(32, 32)  1.51 us

profile of v1, /device:TPU:24, one launch (start us, length us, event | category | flops | bytes accessed | tf_op | source)
XLA Modules:
  0.0 73.9 jit_solution(15170903425290726792)
XLA Ops:
  1.3 0.0 copy-start
  1.3 69.6 %shard_map.86 = (f32[8,128]{1,0:T(8,128)}, f32[8,128]{1,0:T(8,128)}) custom-call(bf16[32,131072]{1,0:T(8,128)(2,1)} %policy_rows.1, bf16[256,16,1024]{2,1,0:T(8,128)(2,1)} %bitcast.11, f32[32,1024]{1,0:T(8,128)} %prev.1, f32[32,8,32]{2,1,0:T(8,128)} %costs.1, s32[1,32]{1,0:T(1,128)} %bitcast.13, s32[1]{0:T(128)S(6)} %copy.19.anchor), custom_call_target="tpu_custom_call" | custom-call | tf_op jit(solution)/shard_map/pallas_call | solution.py:376
  70.9 0.7 %reshape.24 = f32[8,4,32]{2,1,0:T(4,128)S(1)} reshape(f32[8,128]{1,0:T(8,128)} %get-tuple-element.4) | data formatting | bytes 8192 | tf_op jit(solution)/shard_map/reshape | solution.py:415
  71.7 0.7 copy.14
  72.4 0.8 %reshape.26 = f32[8,4,32]{2,1,0:T(4,128)S(1)} reshape(f32[8,128]{1,0:T(8,128)} %get-tuple-element.5) | data formatting | bytes 8192 | tf_op jit(solution)/shard_map/reshape | solution.py:415
  73.1 0.0 copy-done
  73.1 0.1 copy.13
  73.2 0.7 copy.15
  (2 shorter events, 0.0 us)
Async XLA Ops:
  1.3 71.8 %copy-start = (f32[32,32]{1,0:T(8,128)S(1)}, f32[32,32]{1,0:T(8,128)}, u32[]{:S(2)}) copy-start(f32[32,32]{1,0:T(8,128)} %param.12) | copy-start | bytes 12292

commit v2 on v0

v2 whole, which is shorter than its diff:
```python
import functools

import jax
import jax.numpy as jnp
from jax import lax
from jax.experimental import pallas as pl
from jax.experimental.pallas import tpu as pltpu
from jax.sharding import PartitionSpec as P

MESH = pl.DeviceIdType.MESH
F32, BF16 = jnp.float32, jnp.bfloat16
STEPS = ((1, 0, 0), (3, 0, 0), (0, 1, 0), (0, 3, 0), (0, 0, 1), (0, 0, 3))
ORDER = (
    0, 1, 3, 4, 12, 16, 48, 15, 60, 5, 13, 2, 7, 8, 20, 51, 28, 19, 49, 52, 6, 14, 63, 29, 35, 55, 9, 36, 44, 53, 50,
    61, 18, 24, 11, 10, 22, 30, 45, 47, 54, 57, 40, 34, 62, 37, 23, 39, 59, 25, 32, 21, 17, 27, 43, 26, 33, 46, 58, 56,
    31, 38, 41, 42,
)
EVENTS = (
    5101, 9198, 17387, 25580, 33769, 46058, 1005, 13294, 21483, 29676, 37865, 41962, 54262, 107511, 136178, 95216,
    70684, 123892, 1, 9274, 4, 1272, 17457, 66, 29807, 33843, 42223, 9456, 5241, 25650, 3, 1206, 17589, 69, 30008, 65,
    21553, 37939, 67, 46260, 70, 13722, 68, 29941, 46455, 2, -1, 38266, 5, 42297, 13499, 6, 17787, 74, 38525, 15, 10176,
    5759, 18369, 78, 6019, 30338, 22409, 72, 46590, 26558, 18, 10400, 18565, 9, 34364, 1627, 71, 30154, 16, 34815,
    17986, 7, 42429, 11, 1736, 38407, -2, 8, 9732, 73, 38460, 13893, 76, 14081, 42950, 10, 75, -3, 114, 49280, 32900,
    14, 1923, 9863, 5832, 26633, 79, 47046, 12, 13, 77, -4, 24, 18967, 87, 6606, 31193, 39373, 1508, 26058, 46998, 91,
    23250, 39637, 10083, 85, 31051, 80, 17, 81, 82, 19, 83, -5, 86, 14735, 20, 18699, 43539, 97, 48221, 98, 15512,
    27151, 84, 6412, 21, -201, 29, 35664, 32, 19468, 19281, 22, 43412, 90, 14993, 28, 27410, 23, 35277, 2510, 88, 47635,
    -6, 11093, 1814, 23063, 27032, 25, 89, 26, 27, -7, 95, 39892, 56, 45594, 93, 39760, 113, 8294, 47, 20446, 18908,
    101, 7521, 41055, 33, 35929, 106, 48798, 92, 30, 94, 31, -8, -101, 109, 16219, 32608, 60, 29469, 35, 3295, 14179,
    117, 24932, -102, 40, 11813, 20002, 100, 7461, 96, 34, 99, -9, 112, 49186, 38, 36257, 28070, 36, 37, 102, 39, 103,
    -10, -103, 126, 41895, 54, 45479, -104, 104, 41, 105, 42, 43, 107, -11, 44, 108, 45, 46, 110, 111, -12, 48, 49, 50,
    51, 115, -13, -105, 52, 116, 53, 118, 55, 119, -14, 120, 57, 121, 58, 122, 59, 123, -15, 124, 61, 125, 62, 63, 127,
    -16,
)
CHUNKS_DURING = 5
CHUNKS = 8


def hops_of():
    hops = [STEPS[i] for i in range(6)]
    for a in range(6):
        for b in range(a + 1, 6):
            if a // 2 != b // 2:
                hops.append(tuple((p + q) % 4 for p, q in zip(STEPS[a], STEPS[b])))
    return hops


HOPS = hops_of()


def tile4(x):
    x = x + pltpu.roll(x, 64, 1)
    return x + pltpu.roll(x, 32, 1)


def lane_group(rows):
    return lax.broadcasted_iota(jnp.int32, (rows, 128), 1) // 32


def kernel(
    policy_rows, action_rows, prev, costs, policy, targets, anchor, rel_out, q_out,
    prev_buf, cost_buf, policy_buf, target_buf, anchor_buf, blocks, own_rows, actions, column, first_tile, acc, rest,
    cost_part, half_out, half_in, fresh, parts, combined, message, arrived,
    in_sem, rows_sem, other_sem, act_sem, recv_sem, col_sem, half_sem, fresh_sem, q_sem,
    send_sem, psend_sem, csend_sem, hsend_sem, fsend_sem, qsend_sem,
):
    row, col = lax.axis_index("row"), lax.axis_index("col")
    core = row % 2
    z = row // 2 % 4
    y_lo = row // 8
    y_hi, x = col // 4, col % 4
    y = y_hi * 2 + y_lo

    def device(x, y, z, core):
        return ((y % 2 * 4 + z) * 2 + core, y // 2 * 4 + x)

    ways = [device((x + a) % 4, (y + b) % 4, (z + c) % 4, core) for a, b, c in HOPS]
    twin = (row + 1 - 2 * core, col)

    barrier = pltpu.get_barrier_semaphore()
    for other in ways + [twin]:
        pl.semaphore_signal(barrier, inc=1, device_id=other, device_id_type=MESH)

    load_prev = pltpu.make_async_copy(prev, prev_buf, in_sem.at[0])
    load_prev.start()

    def block_of(code, core):
        there = device((x - code // 16) % 4, (y - code // 4 % 4) % 4, (z - code % 4) % 4, core)
        return pl.multiple_of((there[0] * 8 + there[1]) * 1024, 1024)

    for n in range(64):
        pltpu.make_async_copy(
            policy_rows.at[:, pl.ds(block_of(ORDER[n], core), 1024)], own_rows.at[n, pl.ds(0, 32)], rows_sem.at[n // 4]
        ).start()

    small_loads = [
        pltpu.make_async_copy(source, target, in_sem.at[n + 1])
        for n, (source, target) in enumerate(
            ((costs, cost_buf), (policy, policy_buf), (targets, target_buf), (anchor, anchor_buf))
        )
    ]
    for copy in small_loads:
        copy.start()

    load_prev.wait()
    blocks[0] = prev_buf[...].astype(BF16)
    pl.semaphore_wait(barrier, 19)

    def wait_for(ref, sem):
        pltpu.make_async_copy(ref, ref, sem).wait()

    def send_rows():
        for n in range(64):
            pltpu.make_async_remote_copy(
                policy_rows.at[:, pl.ds(block_of(ORDER[n], 1 - core), 1024)], own_rows.at[n, pl.ds(32, 32)],
                psend_sem.at[0], other_sem.at[n // 4], device_id=twin, device_id_type=MESH,
            ).start()
        for n in range(CHUNKS):
            half, part = n % 2, n // 2
            pltpu.make_async_copy(
                action_rows.at[pl.ds(64 * part, 64), pl.ds(8 * half, 8)], actions.at[half, pl.ds(64 * part, 64)],
                act_sem.at[n],
            ).start()

    def part_cost():
        for copy in small_loads:
            copy.wait()
        chosen = policy_buf[...][:, None, :] == lax.broadcasted_iota(jnp.int32, (1, 8, 32), 1)
        cost = jnp.sum(jnp.where(chosen, cost_buf[...], 0.0), axis=1)
        cost_part[...] = jnp.concatenate([cost] * 4, axis=0).T

    def send_block(half, hop, source, target):
        pltpu.make_async_remote_copy(
            blocks.at[source, pl.ds(16 * half, 16)], blocks.at[target, pl.ds(16 * half, 16)],
            send_sem.at[0], recv_sem.at[half * 64 + target], device_id=ways[hop], device_id_type=MESH,
        ).start()

    slot = {code: n for n, code in enumerate(ORDER)}

    def forward_column():
        for n in range(8):
            y_other, z_other = n // 4, n % 4
            code = (y_lo - y_other + 4) % 4 * 4 + (z - z_other + 4) % 4
            where = 0
            for c in range(16):
                if c // 4 != 2:
                    where = where + jnp.where(code == c, slot[c], 0)
            place = n * 2 + core
            pltpu.make_async_remote_copy(
                blocks.at[where], column.at[place], csend_sem.at[0], col_sem.at[1], device_id=twin, device_id_type=MESH
            ).start()
            pltpu.make_async_copy(blocks.at[where], column.at[place], col_sem.at[0]).start()

    def policy_group(g):
        wait_for(own_rows.at[pl.ds(4 * g, 4), pl.ds(0, 32)], rows_sem.at[g])
        wait_for(own_rows.at[pl.ds(4 * g, 4), pl.ds(32, 32)], other_sem.at[g])
        left = own_rows[4 * g : 4 * g + 4].reshape(256, 1024)
        right = blocks[4 * g : 4 * g + 4].reshape(128, 1024)
        out = lax.dot_general(left, right, (((1,), (1,)), ((), ())), preferred_element_type=F32)
        acc[...] = out if g == 0 else acc[...] + out

    has_fresh = col < 4

    def action_chunk(n):
        half, part = n % 2, n // 2
        if n == 0:
            eight = column.at[pl.ds(0, 8)]
            wait_for(eight, col_sem.at[0])
            wait_for(eight, col_sem.at[1])
        here = pl.ds(64 * part, 64)
        wait_for(actions.at[half, here], act_sem.at[n])
        chunk = actions[half, here].reshape(512, 1024)
        values = column[8 * half : 8 * half + 8].reshape(256, 1024)
        out = lax.dot_general(chunk, values, (((1,), (1,)), ((), ())), preferred_element_type=F32)
        out = out.reshape(64, 8, 256)
        mine = lax.broadcasted_iota(jnp.int32, (8, 256), 0)
        theirs = lax.broadcasted_iota(jnp.int32, (8, 256), 1) // 32
        keep = mine == theirs
        if half == 0:
            keep = keep & ((theirs > 0) | jnp.logical_not(has_fresh))
        out = jnp.where(keep[None], out, 0.0)
        out = jnp.sum(out[:, :, 0:128] + out[:, :, 128:256], axis=1)
        if half == 0:
            rest[here] = out

            @pl.when(has_fresh)
            def _():
                pick = (
                    lax.broadcasted_iota(jnp.int32, (64, 512), 1) == 8 * lax.broadcasted_iota(jnp.int32, (64, 512), 0)
                ).astype(BF16)
                first_tile[here] = jnp.dot(pick, chunk, preferred_element_type=F32).astype(BF16)
        else:
            rest[here] = jnp.where(lane_group(64) == 0, tile4(rest[here] + out), 0.0)

    sent = 0
    for event in EVENTS:
        if event >= 1000:
            event, target = divmod(event - 1000, 64)
            event, source = divmod(event, 64)
            send_block(event % 2, event // 2, source, target)
            sent += 1
            if sent == 12:
                send_rows()
                part_cost()
        elif event >= 0:
            half, n = divmod(event, 64)
            wait_for(blocks.at[n, pl.ds(16 * half, 16)], recv_sem.at[event])
        elif event > -100:
            policy_group(-1 - event)
        elif event > -200:
            action_chunk(-101 - event)
        else:
            forward_column()

    group = lane_group(64)
    total = jnp.where(group == 0, acc[0:64, :], 0.0)
    for b in range(1, 4):
        total = jnp.where(group == b, acc[64 * b : 64 * b + 64, :], total)
    total = tile4(total)
    half_out[...] = total[32:64]
    swap = pltpu.make_async_remote_copy(
        half_out, half_in, hsend_sem.at[0], half_sem.at[0], device_id=twin, device_id_type=MESH
    )
    swap.start()
    mine = total[0:32] + cost_part[...]
    swap.wait_recv()
    mine = mine + half_in[...]
    fresh[...] = mine
    group = lane_group(32)
    high = mine.astype(BF16).astype(F32)
    mid = (mine - high).astype(BF16).astype(F32)
    low = mine - high - mid
    parts[...] = jnp.where(
        group == 0, high, jnp.where(group == 1, mid, jnp.where(group == 2, low, 1.0))
    ).astype(BF16)

    place = row % 4 * 8 + col
    target_col = row // 4
    is_target = col == target_col
    for k in range(1, 16):
        pltpu.make_async_remote_copy(
            parts, combined.at[place], fsend_sem.at[0], fresh_sem.at[0],
            device_id=((row + k) % 16, target_col), device_id_type=MESH,
        ).start()

    @pl.when(is_target)
    def _():
        pltpu.make_async_copy(parts, combined.at[place], fresh_sem.at[0]).start()

    @pl.when(jnp.logical_not(is_target))
    def _():
        pltpu.make_async_remote_copy(
            parts, combined.at[place], fsend_sem.at[0], fresh_sem.at[0],
            device_id=(row, target_col), device_id_type=MESH,
        ).start()

    for n in range(CHUNKS_DURING, CHUNKS):
        action_chunk(n)

    @pl.when(has_fresh)
    def _():
        wait_for(combined, fresh_sem.at[0])
        states = col * 1024 + lax.broadcasted_iota(jnp.int32, (8, 1024), 1)
        chosen = (states == anchor_buf[...]).astype(BF16)
        values = combined[...].reshape(1024, 128)
        gain = jnp.dot(chosen, values, preferred_element_type=F32)
        late = jnp.dot(first_tile[...], values, preferred_element_type=F32) + rest[...]
        for c in range(8):
            message[c, 0:32] = late[32 * c : 32 * c + 32]
            message[c, 32:40] = gain

    @pl.when(jnp.logical_not(has_fresh))
    def _():
        for c in range(8):
            message[c, 0:32] = rest[32 * c : 32 * c + 32]
            message[c, 32:40] = jnp.zeros((8, 128), F32)

    for k in range(1, 8):
        other = (col + k) % 8
        pltpu.make_async_remote_copy(
            message.at[other], arrived.at[k - 1], qsend_sem.at[0], q_sem.at[0],
            device_id=(row, other), device_id_type=MESH,
        ).start()
    total = message[col]
    wait_for(arrived, q_sem.at[0])
    for k in range(7):
        total = total + arrived[k]
    gain = tile4(jnp.where(lane_group(8) < 3, total[32:40], 0.0))[0:1]
    total = total[0:32]
    values = tile4(jnp.where(group < 3, total, 0.0))
    weights = tile4(jnp.where(group == 3, total, 0.0))
    both = jnp.where(group == 0, fresh[...] - gain, values - gain * weights - gain).T
    rel_out[...] = both[0:32]
    q_out[...] = both[32:64] + target_buf[...]

    wait_for(blocks.at[pl.ds(0, 63)], send_sem.at[0])
    wait_for(own_rows.at[:, pl.ds(32, 32)], psend_sem.at[0])
    wait_for(column.at[pl.ds(0, 8)], csend_sem.at[0])
    swap.wait_send()

    @pl.when(is_target)
    def _():
        wait_for(combined.at[pl.ds(0, 15)], fsend_sem.at[0])

    @pl.when(jnp.logical_not(is_target))
    def _():
        wait_for(combined.at[pl.ds(0, 16)], fsend_sem.at[0])

    wait_for(arrived, qsend_sem.at[0])


def local(policy_rows, action_rows, prev_values, action_costs, policy, target_costs, anchor):
    any_spec = pl.BlockSpec(memory_space=pl.ANY)
    dma = pltpu.SemaphoreType.DMA
    return pl.pallas_call(
        kernel,
        out_shape=[jax.ShapeDtypeStruct((32, 32), F32)] * 2,
        in_specs=[any_spec] * 7,
        out_specs=[pl.BlockSpec(memory_space=pltpu.VMEM)] * 2,
        scratch_shapes=[
            pltpu.VMEM((32, 1024), F32),
            pltpu.VMEM((32, 8, 32), F32),
            pltpu.VMEM((1, 32), jnp.int32),
            pltpu.VMEM((32, 32), F32),
            pltpu.VMEM((1, 1), jnp.int32),
            pltpu.VMEM((64, 32, 1024), BF16),
            pltpu.VMEM((64, 64, 1024), BF16),
            pltpu.VMEM((2, 256, 8, 1024), BF16),
            pltpu.VMEM((16, 32, 1024), BF16),
            pltpu.VMEM((256, 1024), BF16),
            pltpu.VMEM((256, 128), F32),
            pltpu.VMEM((256, 128), F32),
            pltpu.VMEM((32, 128), F32),
            pltpu.VMEM((32, 128), F32),
            pltpu.VMEM((32, 128), F32),
            pltpu.VMEM((32, 128), F32),
            pltpu.VMEM((32, 128), BF16),
            pltpu.VMEM((32, 32, 128), BF16),
            pltpu.VMEM((8, 40, 128), F32),
            pltpu.VMEM((7, 40, 128), F32),
            dma((5,)), dma((16,)), dma((16,)), dma((8,)), dma((128,)), dma((2,)), dma((1,)), dma((1,)), dma((1,)),
            dma((1,)), dma((1,)), dma((1,)), dma((1,)), dma((1,)), dma((1,)),
        ],
        compiler_params=pltpu.CompilerParams(
            collective_id=0, has_side_effects=True, vmem_limit_bytes=60 * 1024 * 1024
        ),
    )(
        policy_rows,
        action_rows.reshape(action_rows.shape[0], 16, 1024),
        prev_values,
        action_costs,
        policy.reshape(1, 32),
        target_costs,
        anchor.reshape(1, 1),
    )


def solution(mesh):
    in_specs = (
        P(("row", "col"), None),
        P("row", None, "col", None),
        P(None, ("row", "col")),
        P(None, None, ("row", "col")),
        P(("row", "col")),
        P(None, ("row", "col")),
        P(),
    )
    out_specs = (P(None, ("row", "col")), P(None, ("row", "col")))
    return jax.shard_map(local, mesh=mesh, in_specs=in_specs, out_specs=out_specs, check_vma=False)
```

time: 884 us -> 51.6 us (0.06)
  waiting for transfers between devices: 433 us -> 0 us
  blocking collectives: 388 us -> 0 us
  Pallas kernels: 0 us -> 47.4 us
  matrix products: 23.3 us -> 0 us
  local copies, waits for them, and re-layouts: 18.9 us -> 2.65 us
  between operations: 14.4 us -> 1.29 us
    all_gather x2 -> x0, waiting for transfers between devices: 363 us -> none  [the longest x1 343 us: local(): lax.all_gather(prev_bf16, ('row', 'col'), axis=1, tiled=True)]
    all_gather x1 -> x0, blocking collectives: 293 us -> none  [local(): fresh_all = lax.all_gather(fresh_vals, ('row', 'col'), axis=1, tiled=True)]
    psum x1 -> x0, blocking collectives: 95 us -> none  [local(): gain_value = lax.psum(picked, ('row', 'col'))]
    reduce_scatter x1 -> x0, waiting for transfers between devices: 70.2 us -> none  [local(): lax.psum_scatter(partial_value, 'col', scatter_dimension=1, tiled=True)]
    pallas_call x0 -> x1, Pallas kernels: none -> 47.4 us  [local(): pl.pallas_call(kernel, out_shape=[jax.ShapeDtypeStruct((32, 32), F32)] *...]
    dot_general x2 -> x0, matrix products: 23.3 us -> none  [the longest x1 15.7 us: local(): lax.dot_general(lax.all_gather(prev_bf16, ('row', 'col'), axis=1, tiled=T...]
    unnamed x9 -> x2, local copies, waits for them, and re-layouts: 18.8 us -> 2.65 us
  transfers between devices with their start and end apart: 3 -> 0, of which waited for: 3 -> 0; matrix products, arithmetic and copies ran while one was open for 2% -> 0% of each run, Pallas kernels for 0% -> 0%
where the time goes in v2:
time: 51.6 us; the launch traced here: 51.3 us
  Pallas kernels  47.4 us (92%)
  local copies, waits for them, and re-layouts  2.65 us (5%)
  between operations  1.29 us (2%)
    pallas_call x1, Pallas kernels, local(): pl.pallas_call(kernel, out_shape=[jax.ShapeDtypeStruct((32, 32), F32)] *...  47.4 us
    unnamed x2, local copies, waits for them, and re-layouts  2.65 us

profile of v2, /device:TPU:24, one launch (start us, length us, event | category | flops | bytes accessed | tf_op | source)
XLA Modules:
  0.0 51.3 jit_solution(10418234142837184888)
XLA Ops:
  1.3 47.4 %shard_map.86 = (f32[32,32]{1,0:T(8,128)}, f32[32,32]{1,0:T(8,128)}) custom-call(bf16[32,131072]{1,0:T(8,128)(2,1)} %policy_rows.1, bf16[256,16,1024]{2,1,0:T(8,128)(2,1)} %bitcast.4, f32[32,1024]{1,0:T(8,128)} %prev.1, f32[32,8,32]{2,1,0:T(8,128)} %costs.1, s32[1,32]{1,0:T(1,128)} %bitcast.5, f32[32,32]{1,0:T(8,128)} %targets.1, s32[1,1]{1,0:T(1,128)} %bitcast.3.anchor), custom_call_target="tpu_custom_call" | custom-call | tf_op jit(solution)/shard_map/pallas_call | solution.py:314
  48.6 1.3 %copy.12 = f32[32,32]{1,0:T(8,128)} copy(f32[32,32]{1,0:T(8,128)} %get-tuple-element.4) | data formatting | bytes 8192
  50.0 1.3 %copy.13 = f32[32,32]{1,0:T(8,128)} copy(f32[32,32]{1,0:T(8,128)} %get-tuple-element.5) | data formatting | bytes 8192

commit v3 on v2

--- a/solution.py
+++ b/solution.py
@@ -56,10 +56,21 @@
     return lax.broadcasted_iota(jnp.int32, (rows, 128), 1) // 32
 
 
+def pack(x, group):
+    out = x[0:8]
+    for g in range(1, 4):
+        out = jnp.where(group == g, x[8 * g : 8 * g + 8], out)
+    return out
+
+
+def turn(x, groups):
+    return x if groups % 4 == 0 else pltpu.roll(x, groups % 4 * 32, 1)
+
+
 def kernel(
-    policy_rows, action_rows, prev, costs, policy, targets, anchor, rel_out, q_out,
+    policy_rows, action_rows, prev, costs, policy, targets, anchor, rel_out, q_out, gain_out,
     prev_buf, cost_buf, policy_buf, target_buf, anchor_buf, blocks, own_rows, actions, column, first_tile, acc, rest,
-    cost_part, half_out, half_in, fresh, parts, combined, message, arrived,
+    cost_part, half_out, half_in, fresh, packed, gathered, combined, row_sums, message, arrived,
     in_sem, rows_sem, other_sem, act_sem, recv_sem, col_sem, half_sem, fresh_sem, q_sem,
     send_sem, psend_sem, csend_sem, hsend_sem, fsend_sem, qsend_sem,
 ):
@@ -189,7 +200,7 @@
                 ).astype(BF16)
                 first_tile[here] = jnp.dot(pick, chunk, preferred_element_type=F32).astype(BF16)
         else:
-            rest[here] = jnp.where(lane_group(64) == 0, tile4(rest[here] + out), 0.0)
+            rest[here] = tile4(rest[here] + out)
 
     sent = 0
     for event in EVENTS:
@@ -226,30 +237,26 @@
     mine = mine + half_in[...]
     fresh[...] = mine
     group = lane_group(32)
-    high = mine.astype(BF16).astype(F32)
-    mid = (mine - high).astype(BF16).astype(F32)
-    low = mine - high - mid
-    parts[...] = jnp.where(
-        group == 0, high, jnp.where(group == 1, mid, jnp.where(group == 2, low, 1.0))
-    ).astype(BF16)
+    small = lane_group(8)
+    packed[...] = pack(mine, small)
 
     place = row % 4 * 8 + col
     target_col = row // 4
     is_target = col == target_col
     for k in range(1, 16):
         pltpu.make_async_remote_copy(
-            parts, combined.at[place], fsend_sem.at[0], fresh_sem.at[0],
+            packed, gathered.at[place], fsend_sem.at[0], fresh_sem.at[0],
             device_id=((row + k) % 16, target_col), device_id_type=MESH,
         ).start()
 
     @pl.when(is_target)
     def _():
-        pltpu.make_async_copy(parts, combined.at[place], fresh_sem.at[0]).start()
+        pltpu.make_async_copy(packed, gathered.at[place], fresh_sem.at[0]).start()
 
     @pl.when(jnp.logical_not(is_target))
     def _():
         pltpu.make_async_remote_copy(
-            parts, combined.at[place], fsend_sem.at[0], fresh_sem.at[0],
+            packed, gathered.at[place], fsend_sem.at[0], fresh_sem.at[0],
             device_id=(row, target_col), device_id_type=MESH,
         ).start()
 
@@ -258,21 +265,42 @@
 
     @pl.when(has_fresh)
     def _():
-        wait_for(combined, fresh_sem.at[0])
+        sums = lax.dot_general(
+            jnp.ones((8, 1024), BF16), first_tile[...], (((1,), (1,)), ((), ())), preferred_element_type=F32
+        )
+        for c in range(8):
+            row_sums[c] = turn(sums[:, 128 * (c // 4) : 128 * (c // 4) + 128], -c)
+
+    @pl.when(has_fresh)
+    def _():
+        wait_for(gathered, fresh_sem.at[0])
+        for n in range(32):
+            line = gathered[n]
+            high = line.astype(BF16).astype(F32)
+            mid = (line - high).astype(BF16).astype(F32)
+            low = line - high - mid
+            for g in range(4):
+                parts = jnp.where(
+                    small == 0,
+                    turn(high, -g),
+                    jnp.where(small == 1, turn(mid, 1 - g), jnp.where(small == 2, turn(low, 2 - g), 0.0)),
+                )
+                combined[32 * n + 8 * g : 32 * n + 8 * g + 8] = parts.astype(BF16)
         states = col * 1024 + lax.broadcasted_iota(jnp.int32, (8, 1024), 1)
         chosen = (states == anchor_buf[...]).astype(BF16)
-        values = combined[...].reshape(1024, 128)
-        gain = jnp.dot(chosen, values, preferred_element_type=F32)
-        late = jnp.dot(first_tile[...], values, preferred_element_type=F32) + rest[...]
+        gain = jnp.dot(chosen, combined[...], preferred_element_type=F32)
+        late = jnp.dot(first_tile[...], combined[...], preferred_element_type=F32)
+        values = rest[...] + tile4(late)
+        first = lax.broadcasted_iota(jnp.int32, (8, 128), 0) == 0
         for c in range(8):
-            message[c, 0:32] = late[32 * c : 32 * c + 32]
-            message[c, 32:40] = gain
+            message[c, 0:8] = pack(values[32 * c : 32 * c + 32], small)
+            message[c, 8:16] = jnp.where(first, gain, row_sums[c])
 
     @pl.when(jnp.logical_not(has_fresh))
     def _():
         for c in range(8):
-            message[c, 0:32] = rest[32 * c : 32 * c + 32]
-            message[c, 32:40] = jnp.zeros((8, 128), F32)
+            message[c, 0:8] = pack(rest[32 * c : 32 * c + 32], small)
+            message[c, 8:16] = jnp.zeros((8, 128), F32)
 
     for k in range(1, 8):
         other = (col + k) % 8
@@ -284,13 +312,12 @@
     wait_for(arrived, q_sem.at[0])
     for k in range(7):
         total = total + arrived[k]
-    gain = tile4(jnp.where(lane_group(8) < 3, total[32:40], 0.0))[0:1]
-    total = total[0:32]
-    values = tile4(jnp.where(group < 3, total, 0.0))
-    weights = tile4(jnp.where(group == 3, total, 0.0))
-    both = jnp.where(group == 0, fresh[...] - gain, values - gain * weights - gain).T
+    gain = tile4(total[8:16])[0:1]
+    values = jnp.concatenate([turn(total[0:8], 1 - g) for g in range(4)], axis=0)
+    both = jnp.where(group == 0, fresh[...], jnp.where(group == 1, values, gain)).T
     rel_out[...] = both[0:32]
-    q_out[...] = both[32:64] + target_buf[...]
+    gain_out[...] = both[64:96]
+    q_out[...] = both[32:64] - both[64:96] * total[9:10, 0:32] + target_buf[...]
 
     wait_for(blocks.at[pl.ds(0, 63)], send_sem.at[0])
     wait_for(own_rows.at[:, pl.ds(32, 32)], psend_sem.at[0])
@@ -299,11 +326,11 @@
 
     @pl.when(is_target)
     def _():
-        wait_for(combined.at[pl.ds(0, 15)], fsend_sem.at[0])
+        wait_for(gathered.at[pl.ds(0, 15)], fsend_sem.at[0])
 
     @pl.when(jnp.logical_not(is_target))
     def _():
-        wait_for(combined.at[pl.ds(0, 16)], fsend_sem.at[0])
+        wait_for(gathered.at[pl.ds(0, 16)], fsend_sem.at[0])
 
     wait_for(arrived, qsend_sem.at[0])
 
@@ -311,11 +338,11 @@
 def local(policy_rows, action_rows, prev_values, action_costs, policy, target_costs, anchor):
     any_spec = pl.BlockSpec(memory_space=pl.ANY)
     dma = pltpu.SemaphoreType.DMA
-    return pl.pallas_call(
+    fresh, values, gain = pl.pallas_call(
         kernel,
-        out_shape=[jax.ShapeDtypeStruct((32, 32), F32)] * 2,
+        out_shape=[jax.ShapeDtypeStruct((32, 32), F32)] * 3,
         in_specs=[any_spec] * 7,
-        out_specs=[pl.BlockSpec(memory_space=pltpu.VMEM)] * 2,
+        out_specs=[pl.BlockSpec(memory_space=pltpu.VMEM)] * 3,
         scratch_shapes=[
             pltpu.VMEM((32, 1024), F32),
             pltpu.VMEM((32, 8, 32), F32),
@@ -333,10 +360,12 @@
             pltpu.VMEM((32, 128), F32),
             pltpu.VMEM((32, 128), F32),
             pltpu.VMEM((32, 128), F32),
-            pltpu.VMEM((32, 128), BF16),
-            pltpu.VMEM((32, 32, 128), BF16),
-            pltpu.VMEM((8, 40, 128), F32),
-            pltpu.VMEM((7, 40, 128), F32),
+            pltpu.VMEM((8, 128), F32),
+            pltpu.VMEM((32, 8, 128), F32),
+            pltpu.VMEM((1024, 128), BF16),
+            pltpu.VMEM((8, 8, 128), F32),
+            pltpu.VMEM((8, 16, 128), F32),
+            pltpu.VMEM((7, 16, 128), F32),
             dma((5,)), dma((16,)), dma((16,)), dma((8,)), dma((128,)), dma((2,)), dma((1,)), dma((1,)), dma((1,)),
             dma((1,)), dma((1,)), dma((1,)), dma((1,)), dma((1,)), dma((1,)),
         ],
@@ -352,6 +381,7 @@
         target_costs,
         anchor.reshape(1, 1),
     )
+    return fresh - gain, values - gain
 
 
 def solution(mesh):

time: 51.6 us -> 46.9 us (0.909)
  Pallas kernels: 47.4 us -> 44 us
  local copies, waits for them, and re-layouts: 2.65 us -> 0 us
  other arithmetic: 0 us -> 1.37 us
    pallas_call x1, Pallas kernels: 47.4 us -> 44 us  [local(): pl.pallas_call(kernel, out_shape=[jax.ShapeDtypeStruct((32, 32), F32)] *...]
    unnamed x2 -> x0, local copies, waits for them, and re-layouts: 2.65 us -> none
    sub x0 -> x1, other arithmetic: none -> 1.37 us  [local(): return (fresh - gain, values - gain)]
where the time goes in v3:
time: 46.9 us; the launch traced here: 46.7 us
  Pallas kernels  44 us (94%)
  other arithmetic  1.37 us (3%)
  between operations  1.29 us (3%)
    pallas_call x1, Pallas kernels, local(): pl.pallas_call(kernel, out_shape=[jax.ShapeDtypeStruct((32, 32), F32)] *...  44 us
    sub x1, other arithmetic, local(): return (fresh - gain, values - gain)  1.37 us

profile of v3, /device:TPU:24, one launch (start us, length us, event | category | flops | bytes accessed | tf_op | source)
XLA Modules:
  0.0 46.7 jit_solution(15982573446329617657)
XLA Ops:
  1.3 44.0 %shard_map.86 = (f32[32,32]{1,0:T(8,128)}, f32[32,32]{1,0:T(8,128)}, f32[32,32]{1,0:T(8,128)}) custom-call(bf16[32,131072]{1,0:T(8,128)(2,1)} %policy_rows.1, bf16[256,16,1024]{2,1,0:T(8,128)(2,1)} %bitcast.4, f32[32,1024]{1,0:T(8,128)} %prev.1, f32[32,8,32]{2,1,0:T(8,128)} %costs.1, s32[1,32]{1,0:T(1,128)} %bitcast.5, f32[32,32]{1,0:T(8,128)} %targets.1, ...), custom_call_target="tpu_custom_call" | custom-call | tf_op jit(solution)/shard_map/pallas_call | solution.py:341
  45.3 1.4 %fusion = (f32[32,32]{1,0:T(8,128)}, f32[32,32]{1,0:T(8,128)}) fusion(f32[32,32]{1,0:T(8,128)} %get-tuple-element.7, f32[32,32]{1,0:T(8,128)} %get-tuple-element.6, f32[32,32]{1,0:T(8,128)} %get-tuple-element.5), kind=kLoop, calls=%fused_computation | loop fusion | flops 2048 | bytes 20480 | tf_op jit(solution)/shard_map/sub | solution.py:384

commit v4 on v3

--- a/solution.py
+++ b/solution.py
@@ -17,21 +17,20 @@
 )
 EVENTS = (
     5101, 9198, 17387, 25580, 33769, 46058, 1005, 13294, 21483, 29676, 37865, 41962, 54262, 107511, 136178, 95216,
-    70684, 123892, 1, 9274, 4, 1272, 17457, 66, 29807, 33843, 42223, 9456, 5241, 25650, 3, 1206, 17589, 69, 30008, 65,
-    21553, 37939, 67, 46260, 70, 13722, 68, 29941, 46455, 2, -1, 38266, 5, 42297, 13499, 6, 17787, 74, 38525, 15, 10176,
-    5759, 18369, 78, 6019, 30338, 22409, 72, 46590, 26558, 18, 10400, 18565, 9, 34364, 1627, 71, 30154, 16, 34815,
-    17986, 7, 42429, 11, 1736, 38407, -2, 8, 9732, 73, 38460, 13893, 76, 14081, 42950, 10, 75, -3, 114, 49280, 32900,
-    14, 1923, 9863, 5832, 26633, 79, 47046, 12, 13, 77, -4, 24, 18967, 87, 6606, 31193, 39373, 1508, 26058, 46998, 91,
-    23250, 39637, 10083, 85, 31051, 80, 17, 81, 82, 19, 83, -5, 86, 14735, 20, 18699, 43539, 97, 48221, 98, 15512,
-    27151, 84, 6412, 21, -201, 29, 35664, 32, 19468, 19281, 22, 43412, 90, 14993, 28, 27410, 23, 35277, 2510, 88, 47635,
-    -6, 11093, 1814, 23063, 27032, 25, 89, 26, 27, -7, 95, 39892, 56, 45594, 93, 39760, 113, 8294, 47, 20446, 18908,
-    101, 7521, 41055, 33, 35929, 106, 48798, 92, 30, 94, 31, -8, -101, 109, 16219, 32608, 60, 29469, 35, 3295, 14179,
-    117, 24932, -102, 40, 11813, 20002, 100, 7461, 96, 34, 99, -9, 112, 49186, 38, 36257, 28070, 36, 37, 102, 39, 103,
-    -10, -103, 126, 41895, 54, 45479, -104, 104, 41, 105, 42, 43, 107, -11, 44, 108, 45, 46, 110, 111, -12, 48, 49, 50,
-    51, 115, -13, -105, 52, 116, 53, 118, 55, 119, -14, 120, 57, 121, 58, 122, 59, 123, -15, 124, 61, 125, 62, 63, 127,
-    -16,
+    70684, 123892, 1, 9274, 4, 1272, 17457, 66, 29807, 33843, 42223, 9456, 5241, 25650, 65, 21553, 2, 3, 67, -1, 37939,
+    46260, 70, 13722, 1206, 17589, 68, 29941, 46455, 69, 30008, 74, 38525, 15, 10176, 5759, 18369, 38266, 5, 42297,
+    13499, 78, 6019, 6, 17787, 30338, 72, 46590, 22409, 18, 10400, 9, 34364, 1627, 71, 30154, 7, 42429, 11, 1736, 18565,
+    26558, -2, 8, 9732, 73, 38460, 16, 34815, 76, 14081, 17986, 10, 75, -3, 114, 49280, 32900, 14, 1923, 38407, 79,
+    47046, 13893, 12, 13, 77, -4, 24, 18967, 87, 6606, 31193, 39373, 42950, 9863, 5832, 26633, 91, 23250, 80, 17, 81,
+    82, 19, 83, -5, 39637, 86, 14735, 1508, 20, 18699, 26058, 97, 48221, 46998, 84, 21, 85, -201, 10083, 6412, 31051,
+    29, 35664, 32, 19468, 43539, 23, 35277, 98, 15512, 2510, 19281, 27151, 22, -6, 88, 25, 89, 26, 90, 27, -7, 43412,
+    14993, 28, 27410, 93, 39760, 113, 8294, 47, 20446, 95, 39892, 47635, 11093, 1814, 23063, 27032, 92, 30, 94, 31, -8,
+    -101, 33, 35929, 56, 45594, 109, 16219, 101, 7521, 18908, 60, 29469, 41055, 106, 48798, 40, 11813, 35, 3295, 20002,
+    32608, 96, 34, 99, -9, -102, 14179, 100, 7461, 117, 24932, 112, 49186, 38, 36257, 28070, 36, 37, 102, 39, 103, -10,
+    126, 41895, 54, 45479, -103, 104, 41, 105, 42, 43, 107, -11, 44, 108, 45, 46, 110, 111, -12, 48, 49, 50, 51, 115,
+    -13, -104, 52, 116, 53, 118, 55, 119, -14, 120, 57, 121, 58, 122, 59, 123, -15, 124, 61, 125, 62, 63, 127, -16,
 )
-CHUNKS_DURING = 5
+CHUNKS_DURING = 4
 CHUNKS = 8
 
 
@@ -68,7 +67,7 @@
 
 
 def kernel(
-    policy_rows, action_rows, prev, costs, policy, targets, anchor, rel_out, q_out, gain_out,
+    policy_rows, action_rows, prev, costs, policy, targets, anchor, out,
     prev_buf, cost_buf, policy_buf, target_buf, anchor_buf, blocks, own_rows, actions, column, first_tile, acc, rest,
     cost_part, half_out, half_in, fresh, packed, gathered, combined, row_sums, message, arrived,
     in_sem, rows_sem, other_sem, act_sem, recv_sem, col_sem, half_sem, fresh_sem, q_sem,
@@ -166,8 +165,8 @@
         wait_for(own_rows.at[pl.ds(4 * g, 4), pl.ds(32, 32)], other_sem.at[g])
         left = own_rows[4 * g : 4 * g + 4].reshape(256, 1024)
         right = blocks[4 * g : 4 * g + 4].reshape(128, 1024)
-        out = lax.dot_general(left, right, (((1,), (1,)), ((), ())), preferred_element_type=F32)
-        acc[...] = out if g == 0 else acc[...] + out
+        product = lax.dot_general(left, right, (((1,), (1,)), ((), ())), preferred_element_type=F32)
+        acc[...] = product if g == 0 else acc[...] + product
 
     has_fresh = col < 4
 
@@ -181,17 +180,17 @@
         wait_for(actions.at[half, here], act_sem.at[n])
         chunk = actions[half, here].reshape(512, 1024)
         values = column[8 * half : 8 * half + 8].reshape(256, 1024)
-        out = lax.dot_general(chunk, values, (((1,), (1,)), ((), ())), preferred_element_type=F32)
-        out = out.reshape(64, 8, 256)
+        product = lax.dot_general(chunk, values, (((1,), (1,)), ((), ())), preferred_element_type=F32)
+        product = product.reshape(64, 8, 256)
         mine = lax.broadcasted_iota(jnp.int32, (8, 256), 0)
         theirs = lax.broadcasted_iota(jnp.int32, (8, 256), 1) // 32
         keep = mine == theirs
         if half == 0:
             keep = keep & ((theirs > 0) | jnp.logical_not(has_fresh))
-        out = jnp.where(keep[None], out, 0.0)
-        out = jnp.sum(out[:, :, 0:128] + out[:, :, 128:256], axis=1)
+        product = jnp.where(keep[None], product, 0.0)
+        product = jnp.sum(product[:, :, 0:128] + product[:, :, 128:256], axis=1)
         if half == 0:
-            rest[here] = out
+            rest[here] = product
 
             @pl.when(has_fresh)
             def _():
@@ -200,7 +199,7 @@
                 ).astype(BF16)
                 first_tile[here] = jnp.dot(pick, chunk, preferred_element_type=F32).astype(BF16)
         else:
-            rest[here] = tile4(rest[here] + out)
+            rest[here] = tile4(rest[here] + product)
 
     sent = 0
     for event in EVENTS:
@@ -315,9 +314,9 @@
     gain = tile4(total[8:16])[0:1]
     values = jnp.concatenate([turn(total[0:8], 1 - g) for g in range(4)], axis=0)
     both = jnp.where(group == 0, fresh[...], jnp.where(group == 1, values, gain)).T
-    rel_out[...] = both[0:32]
-    gain_out[...] = both[64:96]
-    q_out[...] = both[32:64] - both[64:96] * total[9:10, 0:32] + target_buf[...]
+    out[0:32] = both[0:32]
+    out[64:96] = both[64:96]
+    out[32:64] = both[32:64] - both[64:96] * total[9:10, 0:32] + target_buf[...]
 
     wait_for(blocks.at[pl.ds(0, 63)], send_sem.at[0])
     wait_for(own_rows.at[:, pl.ds(32, 32)], psend_sem.at[0])
@@ -338,11 +337,11 @@
 def local(policy_rows, action_rows, prev_values, action_costs, policy, target_costs, anchor):
     any_spec = pl.BlockSpec(memory_space=pl.ANY)
     dma = pltpu.SemaphoreType.DMA
-    fresh, values, gain = pl.pallas_call(
+    out = pl.pallas_call(
         kernel,
-        out_shape=[jax.ShapeDtypeStruct((32, 32), F32)] * 3,
+        out_shape=jax.ShapeDtypeStruct((96, 32), F32),
         in_specs=[any_spec] * 7,
-        out_specs=[pl.BlockSpec(memory_space=pltpu.VMEM)] * 3,
+        out_specs=pl.BlockSpec(memory_space=pltpu.VMEM),
         scratch_shapes=[
             pltpu.VMEM((32, 1024), F32),
             pltpu.VMEM((32, 8, 32), F32),
@@ -381,7 +380,7 @@
         target_costs,
         anchor.reshape(1, 1),
     )
-    return fresh - gain, values - gain
+    return out[0:32] - out[64:96], out[32:64] - out[64:96]
 
 
 def solution(mesh):

time: 46.9 us -> 46.5 us (level)
  no operation moved by 1% of the time
where the time goes in v4:
time: 46.5 us; the launch traced here: 46.3 us
  Pallas kernels  43.6 us (94%)
  other arithmetic  1.37 us (3%)
  between operations  1.29 us (3%)
    pallas_call x1, Pallas kernels, local(): pl.pallas_call(kernel, out_shape=jax.ShapeDtypeStruct((96, 32), F32), in_...  43.6 us
    sub x1, other arithmetic, local(): return (out[0:32] - out[64:96], out[32:64] - out[64:96])  1.37 us

profile of v4, /device:TPU:24, one launch (start us, length us, event | category | flops | bytes accessed | tf_op | source)
XLA Modules:
  0.0 46.3 jit_solution(12734671043357219339)
XLA Ops:
  1.3 43.6 %shard_map.86 = f32[96,32]{1,0:T(8,128)} custom-call(bf16[32,131072]{1,0:T(8,128)(2,1)} %policy_rows.1, bf16[256,16,1024]{2,1,0:T(8,128)(2,1)} %bitcast.4, f32[32,1024]{1,0:T(8,128)} %prev.1, f32[32,8,32]{2,1,0:T(8,128)} %costs.1, s32[1,32]{1,0:T(1,128)} %bitcast.5, f32[32,32]{1,0:T(8,128)} %targets.1, s32[1,1]{1,0:T(1,128)} %bitcast.3.anchor), custom_call_target="tpu_custom_call" | custom-call | tf_op jit(solution)/shard_map/pallas_call | solution.py:340
  44.9 1.4 %slice_subtract_fusion = (f32[32,32]{1,0:T(8,128)}, f32[32,32]{1,0:T(8,128)}) fusion(f32[96,32]{1,0:T(8,128)} %shard_map.86), kind=kLoop, calls=%fused_computation | loop fusion | flops 2048 | bytes 20480 | tf_op jit(solution)/shard_map/sub | solution.py:383

commit v5 on v4

--- a/solution.py
+++ b/solution.py
@@ -87,7 +87,9 @@
     twin = (row + 1 - 2 * core, col)
 
     barrier = pltpu.get_barrier_semaphore()
-    for other in ways + [twin]:
+    used = sorted({(event - 1000) // 8192 for event in EVENTS if event >= 1000})
+    senders = [device((x - a) % 4, (y - b) % 4, (z - c) % 4, core) for a, b, c in (HOPS[i] for i in used)]
+    for other in senders + [twin]:
         pl.semaphore_signal(barrier, inc=1, device_id=other, device_id_type=MESH)
 
     load_prev = pltpu.make_async_copy(prev, prev_buf, in_sem.at[0])
@@ -113,7 +115,7 @@
 
     load_prev.wait()
     blocks[0] = prev_buf[...].astype(BF16)
-    pl.semaphore_wait(barrier, 19)
+    pl.semaphore_wait(barrier, len(senders) + 1)
 
     def wait_for(ref, sem):
         pltpu.make_async_copy(ref, ref, sem).wait()

time: 46.5 us -> 46.4 us (level)
  no operation moved by 1% of the time
where the time goes in v5:
time: 46.4 us; the launch traced here: 46.3 us
  Pallas kernels  43.6 us (94%)
  other arithmetic  1.37 us (3%)
  between operations  1.29 us (3%)
    pallas_call x1, Pallas kernels, local(): pl.pallas_call(kernel, out_shape=jax.ShapeDtypeStruct((96, 32), F32), in_...  43.6 us
    sub x1, other arithmetic, local(): return (out[0:32] - out[64:96], out[32:64] - out[64:96])  1.37 us

profile of v5, /device:TPU:24, one launch (start us, length us, event | category | flops | bytes accessed | tf_op | source)
XLA Modules:
  0.0 46.3 jit_solution(3123435929948524145)
XLA Ops:
  1.3 43.6 %shard_map.86 = f32[96,32]{1,0:T(8,128)} custom-call(bf16[32,131072]{1,0:T(8,128)(2,1)} %policy_rows.1, bf16[256,16,1024]{2,1,0:T(8,128)(2,1)} %bitcast.4, f32[32,1024]{1,0:T(8,128)} %prev.1, f32[32,8,32]{2,1,0:T(8,128)} %costs.1, s32[1,32]{1,0:T(1,128)} %bitcast.5, f32[32,32]{1,0:T(8,128)} %targets.1, s32[1,1]{1,0:T(1,128)} %bitcast.3.anchor), custom_call_target="tpu_custom_call" | custom-call | tf_op jit(solution)/shard_map/pallas_call | solution.py:342
  44.9 1.4 %slice_subtract_fusion = (f32[32,32]{1,0:T(8,128)}, f32[32,32]{1,0:T(8,128)}) fusion(f32[96,32]{1,0:T(8,128)} %shard_map.86), kind=kLoop, calls=%fused_computation | loop fusion | flops 2048 | bytes 20480 | tf_op jit(solution)/shard_map/sub | solution.py:385
